TPU v7x, 32 devices: a whole 2x2x4 slice. The times are simulated.
32 devices in a mesh: batch: 4 (over x, core), centers: 8 (over z, y).
Axes of the slice: x: 2, y: 2, z: 4, core: 2. Of those that a mesh axis runs over, the one named last changes fastest.
Arguments:
- pool_features: float32 [32768, 128], P(('batch', 'centers')), may hold values from -14 to 14
- pool_targets: float32 [32768, 64], P(('batch', 'centers')), may hold values from -6 to 6
- batch_index: int32 [2048], P(('batch', 'centers')), may hold values from 0 to 1023
- centers: float32 [4096, 128], P('centers'), may hold values from -14 to 14
- weights: float32 [4096, 64], P('centers'), as said below
- eig_vectors: float32 [4096, 1024], P(('batch', 'centers')), may hold values from -0.09375 to 0.09375
- eig_scale: float32 [1024], replicated, may hold values from 0.5 to 4
- nys_owner: int32 [4096, 1], P(('batch', 'centers')), may hold values from 0 to 7; in each aligned block of 128 rows (0 to 127, 128 to 255, ...) at most 32 rows name the same one
- nys_offset: int32 [4096], P(('batch', 'centers')), may hold values from 0 to 511
Outputs:
- residual_out: float32 [2048, 64], P(('batch', 'centers'))
- update: float32 [4096, 64], P('centers')
Inputs may be any that keep to these rules, and one draw needn't show every extreme that they name: `nys_owner`: among the 128 rows of one device no owner is named more than 32 times; on some devices one owner is named exactly 32 times. `weights`: every column sums to zero.
All inputs are finite; a program needn't handle non-finite values.
Results may differ from a plain program's by a relative error of at most 0.0003.
Values sent between devices are 32-bit elements; how exact they have to be, the bound alone decides.
A program may use at most 64 MiB of HBM per device.

v0:
```python
import math
import jax
import jax.numpy as jnp
from jax import lax
from jax.sharding import PartitionSpec as P

DEPTH = 3
epsilon = 1e-06
highest = lax.Precision.HIGHEST


def kernel_rows(row_block, center_block, center_norm):
    inner_prod = (
        lax.dot_general(
            row_block,
            center_block,
            (((1,), (1,)), ((), ())),
            precision=highest,
            preferred_element_type=jnp.float32,
        )
        / row_block.shape[1]
    )
    row_norm = jnp.mean(row_block * row_block, axis=1) + epsilon
    norm_scale = jnp.sqrt(row_norm[:, None] * center_norm[None, :])
    sigma_now = inner_prod
    tangent = inner_prod
    for depth_step in range(DEPTH):
        cosine = sigma_now / norm_scale
        arc_angle = jnp.arccos(cosine)
        remain = (math.pi - arc_angle) / math.pi
        sigma_now = (
            norm_scale
            * (jnp.sqrt(1.0 - cosine * cosine) + (math.pi - arc_angle) * cosine)
            / math.pi
        )
        tangent = sigma_now + tangent * remain
    return tangent


def per_device(
    pool_features,
    pool_targets,
    batch_index,
    centers,
    weights,
    eig_vectors,
    eig_scale,
    nys_owner,
    nys_offset,
):
    local_rows = pool_features[batch_index]
    local_targets = pool_targets[batch_index]
    row_count = local_rows.shape[0]
    group_size = lax.axis_size("centers")
    rows_total = row_count * group_size * lax.axis_size("batch")
    center_count = centers.shape[0]
    outputs = weights.shape[1]
    center_norm = jnp.mean(centers * centers, axis=1) + epsilon
    kernel = kernel_rows(
        lax.all_gather(local_rows, "centers", axis=0, tiled=True), centers, center_norm
    )
    partial_pred = jnp.dot(kernel, weights, precision=highest, preferred_element_type=jnp.float32)
    all_targets = lax.all_gather(local_targets, "centers", axis=0, tiled=True)
    prediction = lax.psum(partial_pred, "centers")
    residual = prediction - all_targets
    own_residual = lax.dynamic_slice_in_dim(
        residual, lax.axis_index("centers") * row_count, row_count, 0
    )
    grads_part = lax.dot_general(
        kernel,
        residual,
        (((0,), (0,)), ((), ())),
        precision=highest,
        preferred_element_type=jnp.float32,
    ) / math.sqrt(rows_total)
    grads = lax.psum(grads_part, "batch")
    owner = nys_owner[:, 0]
    slots = max(2, 2 * owner.shape[0] // group_size)
    owner_hot = (owner[:, None] == jnp.arange(group_size, dtype=jnp.int32)[None, :]).astype(
        jnp.int32
    )
    slot_rank = jnp.sum((jnp.cumsum(owner_hot, axis=0) - owner_hot) * owner_hot, axis=1)
    requests = jnp.zeros((group_size, slots), jnp.int32).at[owner, slot_rank].set(nys_offset)
    received = lax.all_to_all(requests, "centers", split_axis=0, concat_axis=0, tiled=True)
    found = grads[received]
    returned = lax.all_to_all(found, "centers", split_axis=0, concat_axis=0, tiled=True)
    picked_grads = returned[owner, slot_rank]
    coeff_part = lax.dot_general(
        eig_vectors,
        picked_grads,
        (((0,), (0,)), ((), ())),
        precision=highest,
        preferred_element_type=jnp.float32,
    )
    coeff = lax.psum(coeff_part, ("batch", "centers"))
    corr_rows = jnp.dot(
        eig_vectors,
        eig_scale[:, None] * coeff,
        precision=highest,
        preferred_element_type=jnp.float32,
    )
    outgoing = (
        jnp.zeros((group_size, slots, outputs), jnp.float32).at[owner, slot_rank].set(corr_rows)
    )
    incoming = lax.all_to_all(outgoing, "centers", split_axis=0, concat_axis=0, tiled=True)
    corr_part = jnp.zeros((center_count, outputs), jnp.float32).at[received].add(incoming)
    correction = lax.psum(corr_part, "batch")
    return (own_residual, correction - grads)


def solution(mesh):
    placed = (
        P(("batch", "centers"), None),
        P(("batch", "centers"), None),
        P(("batch", "centers")),
        P("centers", None),
        P("centers", None),
        P(("batch", "centers"), None),
        P(),
        P(("batch", "centers"), None),
        P(("batch", "centers")),
    )
    return jax.shard_map(
        per_device,
        mesh=mesh,
        in_specs=placed,
        out_specs=(P(("batch", "centers"), None), P("centers", None)),
        check_vma=False,
    )
```

profile of v0, /device:TPU:0, one launch (start us, length us, event | category | flops | bytes accessed | tf_op | source)
XLA Modules:
  0.0 387.0 jit_solution(5106888059048131326)
XLA Ops:
  7.2 0.0 copy-start
  7.2 0.0 copy-start.6
  7.2 0.7 copy-done.6
  7.9 0.1 fusion.4
  8.0 0.2 reduce_window_sum.11
  8.2 0.2 select_reduce_fusion
  8.3 0.0 copy-start.8
  8.4 0.6 broadcast.104
  9.0 0.1 copy-done.8
  9.0 19.9 %scatter_fusion = s32[8,32]{1,0:T(8,128)} fusion(s32[8,32]{1,0:T(8,128)} %broadcast.104, s32[128]{0:T(128)S(1)} %get-tuple-element.8, s32[128]{0:T(128)S(1)} %copy-done.8), kind=kCustom, calls=%fused_computation.4 | custom fusion | bytes 2560 | tf_op jit(solution)/shard_map/scatter | solution.py:83
  28.9 7.4 %all-to-all-start = ((s32[8,1,32]{2,1,0:T(1,128)}), s32[8,1,32]{2,1,0:T(1,128)S(1)}, u32[]{:S(2)}, u32[]{:S(2)}) async-start(s32[8,1,32]{2,1,0:T(1,128)} %bitcast.4), calls=%async_computation | async-start | bytes 8192 | tf_op jit(solution)/shard_map/all_to_all | solution.py:84
  36.3 0.0 all-reduce.5.cloned.1.call-start
  36.4 0.0 copy-done.9
  36.4 0.1 multiply_reduce_fusion
  36.6 0.6 gather_fusion
  37.2 31.2 %all-gather = f32[512,128]{1,0:T(8,128)S(1)} all-gather(f32[64,128]{1,0:T(8,128)S(1)} %gather_fusion), channel_id=2, replica_groups=mesh['batch'=4,'centers'=8] {'centers'}, dimensions={0}, use_global_device_ids=true | all-gather | bytes 294912 | tf_op jit(solution)/shard_map/all_gather | solution.py:60
  68.4 0.1 multiply_reduce_fusion.1
  68.6 0.0 copy-start.4
  68.6 8.9 %multiply_add_fusion = f32[512,512]{1,0:T(8,128)S(1)} fusion(f32[512,128]{1,0:T(8,128)S(1)} %all-gather, f32[512,128]{1,0:T(8,128)S(1)} %copy-done.3, f32[512]{0:T(512)S(1)} %multiply_add_fusion.1, f32[512]{0:T(512)S(1)} %multiply_add_fusion.2), kind=kOutput, calls=%fused_computation.11 | convolution fusion | flops 414187520 | bytes 1576960 | tf_op jit(solution)/shard_map/dot_general | solution.py:14
  77.5 0.0 copy-start.2
  77.5 1.8 fusion.8
  79.3 0.0 all-reduce.5.cloned.1.call-update
  79.4 0.0 all-reduce.7.cloned.1.call-start
  79.4 0.2 copy.23
  79.6 0.6 gather_fusion.1
  80.2 30.8 %all-gather.1 = f32[512,64]{1,0:T(8,128)S(1)} all-gather(f32[64,64]{1,0:T(8,128)S(1)} %gather_fusion.1), channel_id=3, replica_groups=mesh['batch'=4,'centers'=8] {'centers'}, dimensions={0}, use_global_device_ids=true | all-gather | bytes 147456 | tf_op jit(solution)/shard_map/all_gather | solution.py:63
  111.1 0.1 copy.24
  111.2 0.0 all-to-all-done
  111.2 0.1 reshape.100
  111.3 39.5 %all-reduce.5.cloned.1.call-done = f32[512,64]{0,1:T(8,128)} async-done(((f32[512,64]{0,1:T(8,128)}), f32[512,64]{0,1:T(8,128)}) %all-reduce.5.cloned.1.call-update) | async-done | bytes 131088 | tf_op jit(solution)/shard_map/psum | solution.py:64
  150.8 0.9 sub.36
  151.7 1.5 convolution_multiply_fusion.1
  153.2 0.0 all-reduce.7.cloned.1.call-update
  153.2 0.0 all-reduce.9.cloned.1.call-start
  153.3 31.3 %all-reduce.7.cloned.1.call-done = f32[512,64]{0,1:T(8,128)} async-done(((f32[512,64]{0,1:T(8,128)}), f32[512,64]{0,1:T(8,128)}) %all-reduce.7.cloned.1.call-update) | async-done | bytes 131088 | tf_op jit(solution)/shard_map/psum | solution.py:76
  184.6 1.0 copy.26
  185.6 0.7 gather_fusion.2
  186.3 0.1 reshape.114
  186.5 12.2 %all_to_all.22 = f32[8,1,2048]{2,1,0:T(1,128)S(1)} all-to-all(f32[8,1,2048]{2,1,0:T(1,128)S(1)} %reshape.114), channel_id=1, replica_groups=mesh['batch'=4,'centers'=8] {'centers'}, dimensions={0} | all-to-all | bytes 131072 | tf_op jit(solution)/shard_map/all_to_all | solution.py:86
  198.7 0.5 broadcast.212
  199.2 0.8 reduce
  200.0 0.1 reshape.115
  200.1 1.2 gather_fusion.3
  201.3 0.0 copy-done
  201.3 1.1 convolution_bitcast_fusion
  202.5 0.0 all-reduce.9.cloned.1.call-update
  202.5 123.4 %all-reduce.9.cloned.1.call-done = f32[1024,64]{0,1:T(8,128)} async-done(((f32[1024,64]{0,1:T(8,128)}), f32[1024,64]{0,1:T(8,128)}) %all-reduce.9.cloned.1.call-update) | async-done | bytes 262160 | tf_op jit(solution)/shard_map/psum | solution.py:95
  325.9 1.6 convolution_bitcast_fusion.1
  327.5 0.1 copy.27
  327.7 6.9 %scatter_fusion.1 = f32[8,32,64]{2,1,0:T(8,128)S(1)} fusion(f32[8,32,64]{2,1,0:T(8,128)S(1)} %broadcast_in_dim.8, s32[128]{0:T(128)S(1)} %get-tuple-element.8, f32[128,64]{1,0:T(8,128)S(1)} %copy.27), kind=kCustom, calls=%fused_computation.5 | custom fusion | bytes 99328 | tf_op jit(solution)/shard_map/scatter | solution.py:103
  334.6 0.8 reshape.116
  335.3 4.5 %all-to-all-start.2 = ((f32[8,1,2048]{2,1,0:T(1,128)}), f32[8,1,2048]{2,1,0:T(1,128)S(1)}, u32[]{:S(2)}, u32[]{:S(2)}) async-start(f32[8,1,2048]{2,1,0:T(1,128)} %reshape.116), calls=%async_computation.2 | async-start | bytes 131072 | tf_op jit(solution)/shard_map/all_to_all | solution.py:105
  339.8 0.0 all-reduce.11.cloned.1.call-start
  339.9 6.9 %all-to-all-done.2 = f32[8,1,2048]{2,1,0:T(1,128)S(1)} async-done(((f32[8,1,2048]{2,1,0:T(1,128)}), f32[8,1,2048]{2,1,0:T(1,128)S(1)}, u32[]{:S(2)}, u32[]{:S(2)}) %all-to-all-start.2) | async-done | bytes 65568 | tf_op jit(solution)/shard_map/all_to_all | solution.py:105
  346.7 0.8 reduce.1
  347.6 0.1 reshape.117
  347.6 1.7 scatter_custom_fusion.2
  349.4 0.8 copy.28
  350.2 0.0 all-reduce.11.cloned.1.call-update
  350.2 0.1 constant_dynamic-slice_fusion
  350.3 0.7 copy.29
  351.0 27.9 %all-reduce.11.cloned.1.call-done = f32[512,64]{0,1:T(8,128)} async-done(((f32[512,64]{0,1:T(8,128)}), f32[512,64]{0,1:T(8,128)}) %all-reduce.11.cloned.1.call-update) | async-done | bytes 131088 | tf_op jit(solution)/shard_map/psum | solution.py:107
  378.9 0.0 copy-done.1
  378.9 1.6 sub.38
  (18 shorter events, 0.1 us)
Async XLA Ops:
  7.2 194.2 %copy-start = (f32[128,1024]{1,0:T(8,128)S(1)}, f32[128,1024]{1,0:T(8,128)}, u32[]{:S(2)}) copy-start(f32[128,1024]{1,0:T(8,128)} %param.14) | copy-start | bytes 1572868
  7.2 0.7 copy-start.6
  8.3 0.7 copy-start.8
  9.0 27.4 %copy-start.3 = (f32[512,128]{1,0:T(8,128)S(1)}, f32[512,128]{1,0:T(8,128)}, u32[]{:S(2)}) copy-start(f32[512,128]{1,0:T(8,128)} %param.12) | copy-start | bytes 786436
  9.0 27.6 %copy-start.5 = (f32[1024,128]{1,0:T(8,128)S(1)}, f32[1024,128]{1,0:T(8,128)}, u32[]{:S(2)}) copy-start(f32[1024,128]{1,0:T(8,128)} %param.9) | copy-start | bytes 1572868
  28.9 7.5 %copy-start.9 = (s32[64]{0:T(128)S(1)}, s32[64]{0:T(128)}, u32[]{:S(2)}) copy-start(s32[64]{0:T(128)} %param.11) | copy-start | bytes 772
  28.9 82.3 %all-to-all-start = ((s32[8,1,32]{2,1,0:T(1,128)}), s32[8,1,32]{2,1,0:T(1,128)S(1)}, u32[]{:S(2)}, u32[]{:S(2)}) async-start(s32[8,1,32]{2,1,0:T(1,128)} %bitcast.4), calls=%async_computation | async-start | bytes 8192 | tf_op jit(solution)/shard_map/all_to_all | solution.py:84
  36.3 114.5 %all-reduce.5.cloned.1.call-start = ((), (), s32[]{:S(2)}) async-start(), calls=%async_computation.3 | async-start | bytes 262144 | tf_op jit(solution)/shard_map/psum | solution.py:64
  68.6 8.9 %copy-start.4 = (f32[512,64]{0,1:T(8,128)S(1)}, f32[512,64]{0,1:T(8,128)}, u32[]{:S(2)}) copy-start(f32[512,64]{0,1:T(8,128)} %param.13) | copy-start | bytes 393220
  77.5 1.9 copy-start.2
  79.4 105.2 %all-reduce.7.cloned.1.call-start = ((), (), s32[]{:S(2)}) async-start(), calls=%async_computation.4 | async-start | bytes 262144 | tf_op jit(solution)/shard_map/psum | solution.py:76
  153.2 172.7 %all-reduce.9.cloned.1.call-start = ((), (), s32[]{:S(2)}) async-start(), calls=%async_computation.5 | async-start | bytes 524288 | tf_op jit(solution)/shard_map/psum | solution.py:95
  202.5 123.4 %copy-start.7 = (f32[1024]{0:T(1024)S(1)}, f32[1024]{0:T(1024)}, u32[]{:S(2)}) copy-start(f32[1024]{0:T(1024)} %param.15) | copy-start | bytes 12292
  335.3 11.4 %all-to-all-start.2 = ((f32[8,1,2048]{2,1,0:T(1,128)}), f32[8,1,2048]{2,1,0:T(1,128)S(1)}, u32[]{:S(2)}, u32[]{:S(2)}) async-start(f32[8,1,2048]{2,1,0:T(1,128)} %reshape.116), calls=%async_computation.2 | async-start | bytes 131072 | tf_op jit(solution)/shard_map/all_to_all | solution.py:105
  339.8 39.0 %all-reduce.11.cloned.1.call-start = ((), (), s32[]{:S(2)}) async-start(), calls=%async_computation.6 | async-start | bytes 262144 | tf_op jit(solution)/shard_map/psum | solution.py:107
  350.1 28.7 %copy-start.1 = (f32[512,64]{0,1:T(8,128)S(1)}, f32[512,64]{0,1:T(8,128)}, u32[]{:S(2)}) copy-start(f32[512,64]{0,1:T(8,128)} %all-reduce.7.cloned.1.call-done) | copy-start | bytes 393220
Sparse Core Ops, SparseCore 0:
  79.5 71.2 all-reduce.4
  153.7 30.8 all-reduce.6
  202.6 123.2 all-reduce.8
  350.3 28.5 all-reduce.10
where the time goes:
time: 388 us; the launch traced here: 387 us
  waiting for transfers between devices  229 us (59%)
  blocking collectives  74.3 us (19%)
  local copies, waits for them, and re-layouts  36 us (9%)
  matrix products  14.9 us (4%)
  between operations  14 us (4%)
  starting transfers between devices  12.1 us (3%)
  other arithmetic  6.6 us (2%)
    psum x1, waiting for transfers between devices, per_device(): coeff = lax.psum(coeff_part, ('batch', 'centers'))  123 us
    psum x1, waiting for transfers between devices, per_device(): prediction = lax.psum(partial_pred, 'centers')  39.5 us
    psum x1, waiting for transfers between devices, per_device(): grads = lax.psum(grads_part, 'batch')  31.3 us
    all_gather x1, blocking collectives, per_device(): lax.all_gather(local_rows, 'centers', axis=0, tiled=True)  31.2 us
    all_gather x1, blocking collectives, per_device(): all_targets = lax.all_gather(local_targets, 'centers', axis=0, tiled=True)  30.8 us
    psum x1, waiting for transfers between devices, per_device(): correction = lax.psum(corr_part, 'batch')  27.9 us
    scatter x1, local copies, waits for them, and re-layouts, per_device(): jnp.zeros((group_size, slots), jnp.int32).at[owner, slot_rank]  19.9 us
    all_to_all x1, blocking collectives, per_device(): lax.all_to_all(found, 'centers', split_axis=0, concat_axis=0, tiled=True)  12.2 us
  transfers between devices with their start and end apart: 6, of which 5 were waited for; matrix products, arithmetic and copies ran while one was open for 3% of the time, Pallas kernels for 0%

commit v1 on v0

--- a/solution.py
+++ b/solution.py
@@ -92,7 +92,8 @@
         precision=highest,
         preferred_element_type=jnp.float32,
     )
-    coeff = lax.psum(coeff_part, ("batch", "centers"))
+    blocks = lax.all_gather(coeff_part, ("batch", "centers"))
+    coeff = jnp.sum(blocks, axis=0)
     corr_rows = jnp.dot(
         eig_vectors,
         eig_scale[:, None] * coeff,

time: 388 us -> 323 us (0.83)
  waiting for transfers between devices: 229 us -> 153 us
  local copies, waits for them, and re-layouts: 36 us -> 44.4 us
    psum x1 -> x0, waiting for transfers between devices: 123 us -> none  [per_device(): coeff = lax.psum(coeff_part, ('batch', 'centers'))]
    all_gather x0 -> x1, waiting for transfers between devices: none -> 74.4 us  [per_device(): blocks = lax.all_gather(coeff_part, ('batch', 'centers'))]
    psum x1, waiting for transfers between devices: 39.5 us -> 12.8 us  [per_device(): prediction = lax.psum(partial_pred, 'centers')]
    unnamed x26 -> x21, local copies, waits for them, and re-layouts: 2.76 us -> 10.1 us
  transfers between devices with their start and end apart: 6 -> 6, of which waited for: 5 -> 5; matrix products, arithmetic and copies ran while one was open for 3% -> 7% of each run, Pallas kernels for 0% -> 0%
where the time goes in v1:
time: 323 us; the launch traced here: 322 us
  waiting for transfers between devices  153 us (47%)
  blocking collectives  76 us (24%)
  local copies, waits for them, and re-layouts  44.4 us (14%)
  matrix products  15 us (5%)
  between operations  14 us (4%)
  other arithmetic  9.73 us (3%)
  starting transfers between devices  9.72 us (3%)
    all_gather x1, waiting for transfers between devices, per_device(): blocks = lax.all_gather(coeff_part, ('batch', 'centers'))  74.4 us
    all_gather x1, blocking collectives, per_device(): lax.all_gather(local_rows, 'centers', axis=0, tiled=True)  32.6 us
    psum x1, waiting for transfers between devices, per_device(): grads = lax.psum(grads_part, 'batch')  31.3 us
    all_gather x1, blocking collectives, per_device(): all_targets = lax.all_gather(local_targets, 'centers', axis=0, tiled=True)  31.3 us
    psum x1, waiting for transfers between devices, per_device(): correction = lax.psum(corr_part, 'batch')  27.9 us
    scatter x1, local copies, waits for them, and re-layouts, per_device(): jnp.zeros((group_size, slots), jnp.int32).at[owner, slot_rank]  19.9 us
    psum x1, waiting for transfers between devices, per_device(): prediction = lax.psum(partial_pred, 'centers')  12.8 us
    all_to_all x1, blocking collectives, per_device(): lax.all_to_all(found, 'centers', split_axis=0, concat_axis=0, tiled=True)  12.2 us
  transfers between devices with their start and end apart: 6, of which 5 were waited for; matrix products, arithmetic and copies ran while one was open for 7% of the time, Pallas kernels for 0%

profile of v1, /device:TPU:0, one launch (start us, length us, event | category | flops | bytes accessed | tf_op | source)
XLA Modules:
  0.0 322.2 jit_solution(1715061193122446783)
XLA Ops:
  7.2 0.0 copy-start
  7.2 0.0 all-reduce.4.cloned.1.call-start
  7.2 0.7 compare_select_fusion.3
  7.9 1.6 gather_fusion
  9.6 32.6 %all-gather = f32[512,128]{1,0:T(8,128)S(1)} all-gather(f32[64,128]{1,0:T(8,128)S(1)} %gather_fusion), channel_id=2, replica_groups=mesh['batch'=4,'centers'=8] {'centers'}, dimensions={0}, use_global_device_ids=true | all-gather | bytes 294912 | tf_op jit(solution)/shard_map/all_gather | solution.py:60
  42.1 0.1 multiply_reduce_fusion.1
  42.3 1.1 multiply_reduce_fusion
  43.4 0.0 copy-start.3
  43.4 0.0 copy-start.4
  43.4 0.0 copy-start.6
  43.4 0.0 copy-start.2
  43.4 9.9 %multiply_add_fusion = f32[512,512]{1,0:T(8,128)S(1)} fusion(f32[512,128]{1,0:T(8,128)S(1)} %all-gather, f32[512,128]{1,0:T(8,128)} %param.12, f32[512]{0:T(512)S(1)} %multiply_add_fusion.1, f32[512]{0:T(512)S(1)} %multiply_add_fusion.2), kind=kOutput, calls=%fused_computation.12 | convolution fusion | flops 414187520 | bytes 1576960 | tf_op jit(solution)/shard_map/dot_general | solution.py:14
  53.4 0.0 copy-done.3
  53.4 1.8 fusion.8
  55.2 0.0 all-reduce.4.cloned.1.call-update
  55.2 0.1 fusion.4
  55.3 0.2 reduce_window_sum.11
  55.5 0.2 select_reduce_fusion
  55.7 0.6 broadcast.104
  56.3 19.9 %scatter_fusion = s32[8,32]{1,0:T(8,128)} fusion(s32[8,32]{1,0:T(8,128)} %broadcast.104, s32[128]{0:T(128)S(1)} %get-tuple-element.8, s32[128]{0:T(128)S(1)} %copy-done.6), kind=kCustom, calls=%fused_computation.4 | custom fusion | bytes 2560 | tf_op jit(solution)/shard_map/scatter | solution.py:83
  76.1 5.6 %all-to-all-start = ((s32[8,1,32]{2,1,0:T(1,128)}), s32[8,1,32]{2,1,0:T(1,128)S(1)}, u32[]{:S(2)}, u32[]{:S(2)}) async-start(s32[8,1,32]{2,1,0:T(1,128)} %bitcast.4), calls=%async_computation | async-start | bytes 8192 | tf_op jit(solution)/shard_map/all_to_all | solution.py:84
  81.7 0.0 all-reduce.6.cloned.1.call-start
  81.8 0.2 copy.23
  82.0 0.6 gather_fusion.1
  82.6 31.3 %all-gather.1 = f32[512,64]{1,0:T(8,128)S(1)} all-gather(f32[64,64]{1,0:T(8,128)S(1)} %gather_fusion.1), channel_id=3, replica_groups=mesh['batch'=4,'centers'=8] {'centers'}, dimensions={0}, use_global_device_ids=true | all-gather | bytes 147456 | tf_op jit(solution)/shard_map/all_gather | solution.py:63
  113.8 0.1 copy.24
  114.0 0.0 all-to-all-done
  114.0 0.1 reshape.100
  114.1 12.8 %all-reduce.4.cloned.1.call-done = f32[512,64]{0,1:T(8,128)} async-done(((f32[512,64]{0,1:T(8,128)}), f32[512,64]{0,1:T(8,128)}) %all-reduce.4.cloned.1.call-update) | async-done | bytes 131088 | tf_op jit(solution)/shard_map/psum | solution.py:64
  126.8 0.9 sub.36
  127.8 1.4 convolution_multiply_fusion.1
  129.2 0.0 all-reduce.6.cloned.1.call-update
  129.2 0.0 all-gather.5.cloned.1.call-start
  129.3 31.3 %all-reduce.6.cloned.1.call-done = f32[512,64]{0,1:T(8,128)} async-done(((f32[512,64]{0,1:T(8,128)}), f32[512,64]{0,1:T(8,128)}) %all-reduce.6.cloned.1.call-update) | async-done | bytes 131088 | tf_op jit(solution)/shard_map/psum | solution.py:76
  160.6 1.0 copy.26
  161.7 0.7 gather_fusion.2
  162.4 0.1 reshape.115
  162.5 12.2 %all_to_all.22 = f32[8,1,2048]{2,1,0:T(1,128)S(1)} all-to-all(f32[8,1,2048]{2,1,0:T(1,128)S(1)} %reshape.115), channel_id=1, replica_groups=mesh['batch'=4,'centers'=8] {'centers'}, dimensions={0} | all-to-all | bytes 131072 | tf_op jit(solution)/shard_map/all_to_all | solution.py:86
  174.7 0.5 broadcast.212
  175.2 0.8 reduce
  176.1 0.1 reshape.116
  176.1 1.2 gather_fusion.3
  177.4 1.1 convolution_bitcast_fusion
  178.5 0.0 all-gather.5.cloned.1.call-update
  178.5 74.4 %all-gather.5.cloned.1.call-done = f32[32768,64]{0,1:T(8,128)} async-done(((f32[1024,64]{0,1:T(8,128)}), f32[32768,64]{0,1:T(8,128)}) %all-gather.5.cloned.1.call-update) | async-done | bytes 8388624 | tf_op jit(solution)/shard_map/all_gather | solution.py:95
  252.9 8.1 %copy.30 = f32[8,8,32,1024]{3,2,1,0:T(8,128)S(1)} copy(f32[8,8,32,1024]{3,1,2,0:T(8,128)} %bitcast.38) | data formatting | bytes 16777216
  261.0 0.0 copy-start.5
  261.1 1.5 bitcast_reduce_fusion
  262.6 0.7 convolution_bitcast_fusion.1
  263.2 0.1 copy.27
  263.4 6.9 %scatter_fusion.1 = f32[8,32,64]{2,1,0:T(8,128)S(1)} fusion(f32[8,32,64]{2,1,0:T(8,128)S(1)} %broadcast_in_dim.8, s32[128]{0:T(128)S(1)} %get-tuple-element.8, f32[128,64]{1,0:T(8,128)S(1)} %copy.27), kind=kCustom, calls=%fused_computation.5 | custom fusion | bytes 99328 | tf_op jit(solution)/shard_map/scatter | solution.py:104
  270.3 0.8 reshape.117
  271.0 4.0 %all-to-all-start.2 = ((f32[8,1,2048]{2,1,0:T(1,128)}), f32[8,1,2048]{2,1,0:T(1,128)S(1)}, u32[]{:S(2)}, u32[]{:S(2)}) async-start(f32[8,1,2048]{2,1,0:T(1,128)} %reshape.117), calls=%async_computation.2 | async-start | bytes 131072 | tf_op jit(solution)/shard_map/all_to_all | solution.py:106
  275.0 0.0 all-reduce.8.cloned.1.call-start
  275.1 6.9 %all-to-all-done.2 = f32[8,1,2048]{2,1,0:T(1,128)S(1)} async-done(((f32[8,1,2048]{2,1,0:T(1,128)}), f32[8,1,2048]{2,1,0:T(1,128)S(1)}, u32[]{:S(2)}, u32[]{:S(2)}) %all-to-all-start.2) | async-done | bytes 65568 | tf_op jit(solution)/shard_map/all_to_all | solution.py:106
  281.9 0.8 reduce.1
  282.7 0.1 reshape.118
  282.8 1.7 scatter_custom_fusion.2
  284.5 0.8 copy.28
  285.3 0.0 all-reduce.8.cloned.1.call-update
  285.3 0.1 constant_dynamic-slice_fusion
  285.4 0.7 copy.29
  286.1 27.9 %all-reduce.8.cloned.1.call-done = f32[512,64]{0,1:T(8,128)} async-done(((f32[512,64]{0,1:T(8,128)}), f32[512,64]{0,1:T(8,128)}) %all-reduce.8.cloned.1.call-update) | async-done | bytes 131088 | tf_op jit(solution)/shard_map/psum | solution.py:108
  314.0 1.6 sub.38
  (14 shorter events, 0.1 us)
Async XLA Ops:
  7.2 170.2 %copy-start = (f32[128,1024]{1,0:T(8,128)S(1)}, f32[128,1024]{1,0:T(8,128)}, u32[]{:S(2)}) copy-start(f32[128,1024]{1,0:T(8,128)} %param.14) | copy-start | bytes 1572868
  7.2 119.6 %all-reduce.4.cloned.1.call-start = ((), (), s32[]{:S(2)}) async-start(), calls=%async_computation.3 | async-start | bytes 262144 | tf_op jit(solution)/shard_map/psum | solution.py:64
  43.4 10.0 %copy-start.3 = (f32[512,64]{0,1:T(8,128)S(1)}, f32[512,64]{0,1:T(8,128)}, u32[]{:S(2)}) copy-start(f32[512,64]{0,1:T(8,128)} %param.13) | copy-start | bytes 393220
  43.4 11.8 %copy-start.4 = (s32[128,1]{0,1:T(1,128)S(1)}, s32[128,1]{0,1:T(1,128)}, u32[]{:S(2)}) copy-start(s32[128,1]{0,1:T(1,128)} %param.16) | copy-start | bytes 1540
  43.4 12.9 %copy-start.6 = (s32[128]{0:T(128)S(1)}, s32[128]{0:T(128)}, u32[]{:S(2)}) copy-start(s32[128]{0:T(128)} %param.17) | copy-start | bytes 1540
  43.4 38.3 %copy-start.2 = (f32[1024,64]{0,1:T(8,128)S(1)}, f32[1024,64]{0,1:T(8,128)}, u32[]{:S(2)}) copy-start(f32[1024,64]{0,1:T(8,128)} %param.10) | copy-start | bytes 786436
  76.1 37.8 %all-to-all-start = ((s32[8,1,32]{2,1,0:T(1,128)}), s32[8,1,32]{2,1,0:T(1,128)S(1)}, u32[]{:S(2)}, u32[]{:S(2)}) async-start(s32[8,1,32]{2,1,0:T(1,128)} %bitcast.4), calls=%async_computation | async-start | bytes 8192 | tf_op jit(solution)/shard_map/all_to_all | solution.py:84
  81.7 78.9 %all-reduce.6.cloned.1.call-start = ((), (), s32[]{:S(2)}) async-start(), calls=%async_computation.4 | async-start | bytes 262144 | tf_op jit(solution)/shard_map/psum | solution.py:76
  129.2 123.7 %all-gather.5.cloned.1.call-start = ((), (), s32[]{:S(2)}) async-start(), calls=%async_computation.6 | async-start | bytes 8650752 | tf_op jit(solution)/shard_map/all_gather | solution.py:95
  261.0 1.5 copy-start.5
  261.1 53.0 %copy-start.1 = (f32[512,64]{0,1:T(8,128)S(1)}, f32[512,64]{0,1:T(8,128)}, u32[]{:S(2)}) copy-start(f32[512,64]{0,1:T(8,128)} %all-reduce.6.cloned.1.call-done) | copy-start | bytes 393220
  271.0 10.9 %all-to-all-start.2 = ((f32[8,1,2048]{2,1,0:T(1,128)}), f32[8,1,2048]{2,1,0:T(1,128)S(1)}, u32[]{:S(2)}, u32[]{:S(2)}) async-start(f32[8,1,2048]{2,1,0:T(1,128)} %reshape.117), calls=%async_computation.2 | async-start | bytes 131072 | tf_op jit(solution)/shard_map/all_to_all | solution.py:106
  275.0 39.0 %all-reduce.8.cloned.1.call-start = ((), (), s32[]{:S(2)}) async-start(), calls=%async_computation.5 | async-start | bytes 262144 | tf_op jit(solution)/shard_map/psum | solution.py:108
Sparse Core Ops, SparseCore 0:
  55.3 71.4 all-reduce.3
  129.7 30.8 all-reduce.5
  178.7 74.2 all-gather.4
  285.5 28.5 all-reduce.7
